TPU v7x, 256 devices: a whole 4x4x8 slice. The times are simulated.
256 devices in a mesh: dp: 8 (over z_hi, core), expert: 32 (over z_lo, x, y).
Axes of the slice: x: 4, y: 4, z: 8 (z_hi: 4, z_lo: 2; z = z_hi * 2 + z_lo), core: 2. Of those that a mesh axis runs over, the one named last changes fastest.
Arguments:
- tokens: bfloat16 [32768, 2048], P(('dp', 'expert')), may hold values from -6 to 6
- grad_out: bfloat16 [32768, 768], P(('dp', 'expert')), may hold values from -6 to 6
- expert_ids: int32 [32768, 8], P(('dp', 'expert')), may hold values from 0 to 31, all different within a row; in each aligned block of 128 rows (0 to 127, 128 to 255, ...) at most 36 rows name the same one
- gate_probs: float32 [32768, 8], P(('dp', 'expert')), may hold values from 0.03 to 0.3
- owner: int32 [32], replicated, may hold values from 0 to 31, each once
- partner: int32 [32], replicated, may hold values from 0 to 31, as said below
- weight: bfloat16 [32, 2048, 1536], P('expert', 'dp'), may hold values from -0.125 to 0.125
- first_moment: bfloat16 [32, 2048, 1536], P('expert', 'dp'), may hold values from -5.40625 to 5.40625
- second_moment: bfloat16 [32, 2048, 1536], P('expert', 'dp'), may hold values from 4.09375 to 40.75
Outputs:
- adam_step: float32 [32, 2048, 1536], P('expert', 'dp')
Inputs may be any that keep to these rules, and one draw needn't show every extreme that they name: `expert_ids`: among the choices of one device's 128 tokens (aligned blocks of tokens) no expert is named more than 36 times, a bound that some block reaches; a token names 8 different experts. `owner`: each slot appears once. partner[i] is i or (i + 16) % 32, partner[partner[i]] = i, and at least one pair differs.
All inputs are finite; a program needn't handle non-finite values.
Results may differ from a plain program's by a relative error of at most 0.007.
Values may be sent and summed in bfloat16 or wider, within the bound.
A program may use at most 128 MiB of HBM per device.

v0:
```python
import jax
import jax.numpy as jnp
from jax import lax
from jax.sharding import PartitionSpec as P

BETA_ONE = 0.9
BETA_TWO = 0.95
EPSILON = 1e-08


def from_partner(value, axis, bit):
    mask = 2**bit
    pairs = [(source, source ^ mask) for source in range(lax.axis_size(axis))]
    return lax.ppermute(value, axis, pairs)


def routed_rows(tokens, grad_out, expert_ids, gate_probs, dest_table, peers, capacity):
    width = tokens.shape[1]
    grad_width = grad_out.shape[1]
    top_k = expert_ids.shape[1]
    labels = jnp.arange(dest_table.shape[0], dtype=jnp.int32)
    flat_ids = expert_ids.reshape(-1)
    onehot = (flat_ids[:, None] == labels[None, :]).astype(jnp.int32)
    ranks = jnp.sum((jnp.cumsum(onehot, axis=0) - onehot) * onehot, axis=1)
    target = jnp.sum(onehot * dest_table[None, :], axis=1)
    position = target * capacity + ranks
    x_rows = jnp.repeat(tokens, top_k, axis=0)
    g_rows = (
        (gate_probs[:, :, None] * grad_out[:, None, :].astype(jnp.float32))
        .astype(jnp.bfloat16)
        .reshape(-1, grad_width)
    )
    x_buf = (
        jnp.zeros((peers * capacity, width), jnp.bfloat16)
        .at[position]
        .set(x_rows)
        .reshape(peers, capacity, width)
    )
    g_buf = (
        jnp.zeros((peers * capacity, grad_width), jnp.bfloat16)
        .at[position]
        .set(g_rows)
        .reshape(peers, capacity, grad_width)
    )
    return (x_buf, g_buf)


def body(
    tokens, grad_out, expert_ids, gate_probs, owner, partner, weight, first_moment, second_moment
):
    peers = lax.axis_size("expert")
    my_index = lax.axis_index("expert")
    swap_bit = peers.bit_length() - 2
    top_k = expert_ids.shape[1]
    expert_count = owner.shape[0]
    capacity = tokens.shape[0] * top_k * 9 // (8 * expert_count)
    width_hidden = weight.shape[2] // 2
    width = tokens.shape[1]
    labels = jnp.arange(expert_count, dtype=jnp.int32)
    moved = jnp.sum(jnp.where(labels == my_index, partner, 0)) != my_index
    owner_hit = (owner[:, None] == labels[None, :]).astype(jnp.int32)
    dest_table = jnp.sum(owner_hit * partner[None, :], axis=1)
    stacked = jnp.concatenate((weight, first_moment, second_moment), axis=0)
    arrived = from_partner(stacked, "expert", swap_bit)
    stacked = jnp.where(moved, arrived, stacked)
    own_weight = stacked[0:1]
    own_first = stacked[1]
    own_second = stacked[2]
    x_buf, g_buf = routed_rows(
        tokens, grad_out, expert_ids, gate_probs, dest_table, peers, capacity
    )
    x_recv, g_recv = (
        lax.all_to_all(x_buf, "expert", split_axis=0, concat_axis=0, tiled=True),
        lax.all_to_all(g_buf, "expert", split_axis=0, concat_axis=0, tiled=True),
    )
    rows_in = x_recv.reshape(-1, width)
    rows_grad = g_recv.reshape(-1, g_recv.shape[2])
    x_cols = rows_in
    pre_act = jnp.dot(
        x_cols,
        lax.all_gather(own_weight, "dp", axis=1, tiled=True)[0],
        preferred_element_type=jnp.float32,
    )
    back = rows_grad.astype(jnp.float32)
    gate_part = pre_act[:, :width_hidden]
    up_part = pre_act[:, width_hidden:]
    sigma = jax.nn.sigmoid(gate_part)
    silu_value = gate_part * sigma
    slope = sigma * (1.0 + gate_part * (1.0 - sigma))
    delta = jnp.concatenate([back * up_part * slope, back * silu_value], axis=1).astype(
        jnp.bfloat16
    )
    x_cols = rows_in
    contract = (((0,), (0,)), ((), ()))
    grads = lax.psum_scatter(
        lax.dot_general(x_cols, delta, contract, preferred_element_type=jnp.float32).astype(
            jnp.bfloat16
        ),
        "dp",
        scatter_dimension=0,
        tiled=True,
    ).astype(jnp.float32)
    first_new = BETA_ONE * own_first.astype(jnp.float32) + (1.0 - BETA_ONE) * grads
    second_new = BETA_TWO * own_second.astype(jnp.float32) + (1.0 - BETA_TWO) * grads * grads
    step = first_new / (jnp.sqrt(second_new) + EPSILON)
    return step[None]


def solution(mesh):
    in_specs = (
        P(("dp", "expert"), None),
        P(("dp", "expert"), None),
        P(("dp", "expert"), None),
        P(("dp", "expert"), None),
        P(),
        P(),
        P("expert", "dp", None),
        P("expert", "dp", None),
        P("expert", "dp", None),
    )
    out_specs = P("expert", "dp", None)
    return jax.shard_map(body, mesh=mesh, in_specs=in_specs, out_specs=out_specs, check_vma=False)
```

profile of v0, /device:TPU:28, one launch (start us, length us, event | category | flops | bytes accessed | tf_op | source)
XLA Modules:
  0.0 321.0 jit_solution(16407933089594187483)
XLA Ops:
  6.6 2.2 constant_dynamic-update-slice_fusion.2
  8.8 2.1 constant_dynamic-update-slice_fusion.1
  10.8 0.9 constant_dynamic-update-slice_fusion
  11.8 1.9 collective-permute-start
  13.7 0.1 copy.15
  13.8 0.1 eq.53
  14.0 9.0 %reduce-window.6 = s32[32,8,128]{2,1,0:T(8,128)S(1)} reduce-window(s32[32,8,128]{2,1,0:T(8,128)S(1)} %fusion.26, s32[]{:T(128)} %constant.12.clone.1), window={size=1x1x128 pad=0_0x0_0x127_0}, to_apply=%region_3.4 | reduce-window | flops 4161536 | bytes 262148 | tf_op jit(solution)/shard_map/reduce-window
  23.1 0.1 copy.17
  23.4 0.1 copy.19
  23.5 0.1 mul.112
  23.6 0.2 select_reduce_fusion.1
  23.8 0.1 broadcast_add_fusion
  24.0 6.1 %scatter_custom_fusion.1 = bf16[1152,768]{1,0:T(8,128)(2,1)S(1)} fusion(s32[1024]{0:T(1024)S(1)} %bitcast.42, f32[128,768]{1,0:T(8,128)S(1)} %convert_element_type.40, f32[1024]{0:T(1024)S(1)} %mul.112, bf16[]{:T(256)} %constant.14.clone.1), kind=kCustom, calls=%fused_computation.28 | custom fusion | flops 1572864 | bytes 2166786 | tf_op jit(solution)/shard_map/scatter | solution.py:42
  30.1 1.5 reshape.78
  31.6 7.3 %all-to-all-start.1 = ((bf16[32,36,768]{2,1,0:T(8,128)(2,1)}), bf16[32,36,768]{2,1,0:T(8,128)(2,1)}, u32[]{:S(2)}, u32[]{:S(2)}) async-start(bf16[32,36,768]{2,1,0:T(8,128)(2,1)} %reshape.78), calls=%async_computation.1 | async-start | bytes 3932160 | tf_op jit(solution)/shard_map/all_to_all | solution.py:74
  39.0 0.6 fusion.27
  40.2 25.9 %collective-permute-done = bf16[3,256,1536]{2,1,0:T(8,128)(2,1)} collective-permute-done((bf16[3,256,1536]{2,1,0:T(8,128)(2,1)}, bf16[3,256,1536]{2,1,0:T(8,128)(2,1)}, u32[]{:S(2)}, u32[]{:S(2)}) %collective-permute-start) | collective-permute-done | bytes 2359328 | tf_op jit(solution)/shard_map/ppermute | solution.py:14
  66.2 1.9 broadcast_select_fusion
  68.1 0.9 slice.31
  69.1 9.4 %scatter_custom_fusion = bf16[1152,2048]{1,0:T(8,128)(2,1)} fusion(s32[1024]{0:T(1024)S(1)} %bitcast.43, bf16[]{:T(256)} %constant.14.clone.1, bf16[128,2048]{1,0:T(8,128)(2,1)S(1)} %copy-done), kind=kCustom, calls=%fused_computation.5 | custom fusion | bytes 5242882 | tf_op jit(solution)/shard_map/scatter | solution.py:36
  78.4 7.3 %reshape.76 = bf16[32,36,2048]{2,1,0:T(8,128)(2,1)} reshape(bf16[1152,2048]{1,0:T(8,128)(2,1)} %scatter_custom_fusion) | data formatting | bytes 9437184 | tf_op jit(solution)/shard_map/reshape | solution.py:37
  85.7 0.6 all-to-all-done.1
  86.3 8.8 %all-to-all-start = ((bf16[32,36,2048]{2,1,0:T(8,128)(2,1)}), bf16[32,36,2048]{2,1,0:T(8,128)(2,1)}, u32[]{:S(2)}, u32[]{:S(2)}) async-start(bf16[32,36,2048]{2,1,0:T(8,128)(2,1)} %reshape.76), calls=%async_computation | async-start | bytes 10485760 | tf_op jit(solution)/shard_map/all_to_all | solution.py:73
  95.1 3.9 %reshape.79 = f32[1152,768]{1,0:T(8,128)} reshape(bf16[32,36,768]{2,1,0:T(8,128)(2,1)} %all-to-all-done.1) | data formatting | bytes 5308416 | tf_op jit(solution)/shard_map/convert_element_type | solution.py:84
  99.1 99.7 %all-to-all-done = bf16[32,36,2048]{2,1,0:T(8,128)(2,1)} async-done(((bf16[32,36,2048]{2,1,0:T(8,128)(2,1)}), bf16[32,36,2048]{2,1,0:T(8,128)(2,1)}, u32[]{:S(2)}, u32[]{:S(2)}) %all-to-all-start) | async-done | bytes 4718624 | tf_op jit(solution)/shard_map/all_to_all | solution.py:73
  198.7 7.3 %reshape.77 = bf16[1152,2048]{1,0:T(8,128)(2,1)} reshape(bf16[32,36,2048]{2,1,0:T(8,128)(2,1)} %all-to-all-done) | data formatting | bytes 9437184 | tf_op jit(solution)/shard_map/reshape | solution.py:76
  206.0 11.2 %fusion = f32[1152,1536]{1,0:T(8,128)S(1)} fusion(bf16[1152,2048]{1,0:T(8,128)(2,1)} %reshape.77, bf16[1,2048,1536]{2,1,0:T(8,128)(2,1)} %all-gather.2.cloned.1.call-done), kind=kOutput, calls=%fused_computation.3 | convolution fusion | flops 7247757312 | bytes 18087936 | tf_op jit(solution)/shard_map/dot_general | solution.py:79
  217.3 2.1 fusion.5
  219.4 0.2 copy-done.2
  219.6 10.6 %convolution_convert_fusion = bf16[2048,1536]{1,0:T(8,128)(2,1)} fusion(bf16[1152,2048]{1,0:T(8,128)(2,1)S(1)} %copy-done.2, bf16[1152,768]{1,0:T(8,128)(2,1)S(1)} %get-tuple-element.8, bf16[1152,768]{1,0:T(8,128)(2,1)S(1)} %get-tuple-element.7), kind=kOutput, calls=%fused_computation.2 | convolution fusion | flops 7257980928 | bytes 14548992 | tf_op jit(solution)/shard_map/dot_general | solution.py:96
  230.2 80.6 %reduce-scatter.2.cloned.1.call-done = bf16[256,1536]{1,0:T(8,128)(2,1)} async-done(((bf16[2048,1536]{1,0:T(8,128)(2,1)}), bf16[256,1536]{1,0:T(8,128)(2,1)}) %reduce-scatter.2.cloned.1.call-update) | async-done | bytes 786448 | tf_op jit(solution)/shard_map/reduce_scatter | solution.py:95
  310.8 3.3 %fusion.14 = f32[1,256,1536]{2,1,0:T(8,128)} fusion(bf16[256,1536]{1,0:T(8,128)(2,1)} %reduce-scatter.2.cloned.1.call-done, bf16[3,256,1536]{2,1,0:T(8,128)(2,1)S(1)} %broadcast_select_fusion), kind=kLoop, calls=%fused_computation.24 | loop fusion | flops 4718592 | bytes 3932160 | tf_op jit(solution)/shard_map/broadcast_in_dim | solution.py:106
  (32 shorter events, 0.6 us)
Async XLA Ops:
  6.5 62.5 %copy-start = (bf16[128,2048]{1,0:T(8,128)(2,1)S(1)}, bf16[128,2048]{1,0:T(8,128)(2,1)}, u32[]{:S(2)}) copy-start(bf16[128,2048]{1,0:T(8,128)(2,1)} %param.9) | copy-start | bytes 1572868
  6.5 4.3 %copy-start.3 = (bf16[1,256,1536]{2,1,0:T(8,128)(2,1)S(1)}, bf16[1,256,1536]{2,1,0:T(8,128)(2,1)}, u32[]{:S(2)}) copy-start(bf16[1,256,1536]{2,1,0:T(8,128)(2,1)} %param.17) | copy-start | bytes 2359300
  6.5 7.1 %copy-start.5 = (s32[128,8]{0,1:T(8,128)S(1)}, s32[128,8]{0,1:T(8,128)}, u32[]{:S(2)}) copy-start(s32[128,8]{0,1:T(8,128)} %param.11) | copy-start | bytes 12292
  6.5 16.8 %copy-start.4 = (bf16[128,768]{1,0:T(8,128)(2,1)S(1)}, bf16[128,768]{1,0:T(8,128)(2,1)}, u32[]{:S(2)}) copy-start(bf16[128,768]{1,0:T(8,128)(2,1)} %param.10) | copy-start | bytes 589828
  6.5 16.8 %copy-start.6 = (f32[128,8]{0,1:T(8,128)S(1)}, f32[128,8]{0,1:T(8,128)}, u32[]{:S(2)}) copy-start(f32[128,8]{0,1:T(8,128)} %param.12) | copy-start | bytes 12292
  6.5 17.0 %copy-start.7 = (s32[32]{0:T(128)S(1)}, s32[32]{0:T(128)}, u32[]{:S(2)}) copy-start(s32[32]{0:T(128)} %param.13) | copy-start | bytes 388
  6.6 17.0 %copy-start.8 = (s32[32]{0:T(128)S(1)}, s32[32]{0:T(128)}, u32[]{:S(2)}) copy-start(s32[32]{0:T(128)} %param.14) | copy-start | bytes 388
  11.8 54.4 %collective-permute-start = (bf16[3,256,1536]{2,1,0:T(8,128)(2,1)}, bf16[3,256,1536]{2,1,0:T(8,128)(2,1)}, u32[]{:S(2)}, u32[]{:S(2)}) collective-permute-start(bf16[3,256,1536]{2,1,0:T(8,128)(2,1)} %constant_dynamic-update-slice_fusion), channel_id=1, source_target_pairs={{0,16},{1,17},{2,18},{3,19},{4,20},{5,21},{6,22},{7,23},{8,24},{9,... | collective-permute-start | bytes 7077896 | tf_op jit(solution)/shard_map/ppermute | solution.py:14
  31.6 54.7 %all-to-all-start.1 = ((bf16[32,36,768]{2,1,0:T(8,128)(2,1)}), bf16[32,36,768]{2,1,0:T(8,128)(2,1)}, u32[]{:S(2)}, u32[]{:S(2)}) async-start(bf16[32,36,768]{2,1,0:T(8,128)(2,1)} %reshape.78), calls=%async_computation.1 | async-start | bytes 3932160 | tf_op jit(solution)/shard_map/all_to_all | solution.py:74
  38.9 167.1 %all-gather.2.cloned.1.call-start = ((), (), s32[]{:S(2)}) async-start(), calls=%async_computation.3 | async-start | bytes 7077888 | tf_op jit(solution)/shard_map/all_gather | solution.py:81
  86.3 112.4 %all-to-all-start = ((bf16[32,36,2048]{2,1,0:T(8,128)(2,1)}), bf16[32,36,2048]{2,1,0:T(8,128)(2,1)}, u32[]{:S(2)}, u32[]{:S(2)}) async-start(bf16[32,36,2048]{2,1,0:T(8,128)(2,1)} %reshape.76), calls=%async_computation | async-start | bytes 10485760 | tf_op jit(solution)/shard_map/all_to_all | solution.py:73
  95.1 215.7 %reduce-scatter.2.cloned.1.call-start = ((), (), s32[]{:S(2)}) async-start(), calls=%async_computation.4 | async-start | bytes 7077888 | tf_op jit(solution)/shard_map/reduce_scatter | solution.py:95
  206.0 11.2 %copy-start.1 = (f32[1152,768]{1,0:T(8,128)S(1)}, f32[1152,768]{1,0:T(8,128)}, u32[]{:S(2)}) copy-start(f32[1152,768]{1,0:T(8,128)} %reshape.79) | copy-start | bytes 10616836
  217.2 2.3 copy-start.2
Sparse Core Ops, SparseCore 0:
  69.2 96.3 all-gather.1
  230.3 80.4 reduce-scatter.1
where the time goes:
time: 322 us; the launch traced here: 321 us
  waiting for transfers between devices  207 us (64%)
  local copies, waits for them, and re-layouts  36.5 us (11%)
  other arithmetic  23.5 us (7%)
  matrix products  21.8 us (7%)
  starting transfers between devices  18.1 us (6%)
  between operations  14.3 us (4%)
    all_to_all x1, waiting for transfers between devices, body(): lax.all_to_all(x_buf, 'expert', split_axis=0, concat_axis=0, tiled=True)  99.7 us
    reduce_scatter x1, waiting for transfers between devices, body(): lax.psum_scatter(lax.dot_general(x_cols, delta, contract, preferred_eleme...  80.6 us
    ppermute x1, waiting for transfers between devices, from_partner(): return lax.ppermute(value, axis, pairs)  25.9 us
    another operation x4, other arithmetic  11.2 us
    dot_general x1, matrix products, body(): jnp.dot(x_cols, lax.all_gather(own_weight, 'dp', axis=1, tiled=True)[0],...  11.2 us
    dot_general x1, matrix products, body(): lax.dot_general(x_cols, delta, contract, preferred_element_type=jnp.float32)  10.6 us
    scatter x1, local copies, waits for them, and re-layouts, routed_rows(): x_buf = jnp.zeros((peers * capacity, width), jnp.bfloat16).at[position].s...  9.35 us
    all_to_all x1, starting transfers between devices, body(): lax.all_to_all(x_buf, 'expert', split_axis=0, concat_axis=0, tiled=True)  8.79 us
  transfers between devices with their start and end apart: 5, of which 4 were waited for; matrix products, arithmetic and copies ran while one was open for 15% of the time, Pallas kernels for 0%

commit v1 on v0

v1 whole, which is shorter than its diff:
```python
import jax
import jax.numpy as jnp
from jax import lax
from jax.sharding import PartitionSpec as P

BETA_ONE = 0.9
BETA_TWO = 0.95
EPSILON = 1e-08


def from_partner(value, axis, bit):
    mask = 2**bit
    pairs = [(source, source ^ mask) for source in range(lax.axis_size(axis))]
    return lax.ppermute(value, axis, pairs)


def routed_rows(tokens, grad_out, slots, gate_probs, peers, capacity):
    count, width = tokens.shape
    labels = jnp.arange(peers, dtype=jnp.int32)
    hit = slots[None, :, :] == labels[:, None, None]
    chosen = jnp.any(hit, axis=2)
    gates = jnp.sum(jnp.where(hit, gate_probs[None], 0.0), axis=2)
    before = jnp.arange(count)[:, None] < jnp.arange(count)[None, :]
    ranks = jnp.dot(
        chosen.astype(jnp.bfloat16), before.astype(jnp.bfloat16), preferred_element_type=jnp.float32
    ).astype(jnp.int32)
    ranks = jnp.where(chosen, ranks, -1)
    picks = ranks[:, None, :] == jnp.arange(capacity, dtype=jnp.int32)[None, :, None]
    row_gate = jnp.sum(jnp.where(picks, gates[:, None, :], 0.0), axis=2)
    picks = picks.astype(jnp.bfloat16)
    x_buf = jnp.einsum("brt,td->brd", picks, tokens, preferred_element_type=jnp.float32)
    g_buf = jnp.einsum("brt,td->brd", picks, grad_out, preferred_element_type=jnp.float32)
    return x_buf.astype(jnp.bfloat16), (g_buf * row_gate[:, :, None]).astype(jnp.bfloat16)


def body(
    tokens, grad_out, expert_ids, gate_probs, owner, partner, weight, first_moment, second_moment
):
    peers = lax.axis_size("expert")
    my_index = lax.axis_index("expert")
    swap_bit = peers.bit_length() - 2
    top_k = expert_ids.shape[1]
    expert_count = owner.shape[0]
    capacity = tokens.shape[0] * top_k * 9 // (8 * expert_count)
    width_hidden = weight.shape[2] // 2
    width = tokens.shape[1]
    labels = jnp.arange(expert_count, dtype=jnp.int32)
    moved = jnp.sum(jnp.where(labels == my_index, partner, 0)) != my_index
    slots = jnp.sum(jnp.where(expert_ids[:, :, None] == labels, owner, 0), axis=2)
    x_buf, g_buf = routed_rows(tokens, grad_out, slots, gate_probs, peers, capacity)
    x_recv, g_recv = (
        lax.all_to_all(x_buf, "expert", split_axis=0, concat_axis=0, tiled=True),
        lax.all_to_all(g_buf, "expert", split_axis=0, concat_axis=0, tiled=True),
    )
    rows_in = x_recv.reshape(-1, width)
    rows_grad = g_recv.reshape(-1, g_recv.shape[2])
    pre_act = jnp.dot(
        rows_in,
        lax.all_gather(weight, "dp", axis=1, tiled=True)[0],
        preferred_element_type=jnp.float32,
    )
    back = rows_grad.astype(jnp.float32)
    gate_part = pre_act[:, :width_hidden]
    up_part = pre_act[:, width_hidden:]
    sigma = jax.nn.sigmoid(gate_part)
    silu_value = gate_part * sigma
    slope = sigma * (1.0 + gate_part * (1.0 - sigma))
    delta = jnp.concatenate([back * up_part * slope, back * silu_value], axis=1).astype(
        jnp.bfloat16
    )
    contract = (((0,), (0,)), ((), ()))
    grads = lax.psum_scatter(
        lax.dot_general(rows_in, delta, contract, preferred_element_type=jnp.float32).astype(
            jnp.bfloat16
        ),
        "dp",
        scatter_dimension=0,
        tiled=True,
    ).astype(jnp.float32)
    first_new = BETA_ONE * first_moment[0].astype(jnp.float32) + (1.0 - BETA_ONE) * grads
    second_new = BETA_TWO * second_moment[0].astype(jnp.float32) + (1.0 - BETA_TWO) * grads * grads
    step = first_new / (jnp.sqrt(second_new) + EPSILON)
    arrived = from_partner(step.astype(jnp.bfloat16), "expert", swap_bit)
    return jnp.where(moved, arrived.astype(jnp.float32), step)[None]


def solution(mesh):
    in_specs = (
        P(("dp", "expert"), None),
        P(("dp", "expert"), None),
        P(("dp", "expert"), None),
        P(("dp", "expert"), None),
        P(),
        P(),
        P("expert", "dp", None),
        P("expert", "dp", None),
        P("expert", "dp", None),
    )
    out_specs = P("expert", "dp", None)
    return jax.shard_map(body, mesh=mesh, in_specs=in_specs, out_specs=out_specs, check_vma=False)
```

time: 322 us -> 297 us (0.922)
  local copies, waits for them, and re-layouts: 36.5 us -> 9.39 us
  other arithmetic: 23.5 us -> 11.2 us
  matrix products: 21.8 us -> 28.7 us
    all_to_all x1, waiting for transfers between devices: 0.56 us -> 31.3 us  [body(): lax.all_to_all(g_buf, 'expert', split_axis=0, concat_axis=0, tiled=True)]
    all_to_all x1, waiting for transfers between devices: 99.7 us -> 81 us  [body(): lax.all_to_all(x_buf, 'expert', split_axis=0, concat_axis=0, tiled=True)]
    ppermute x1, waiting for transfers between devices: 25.9 us -> 13.2 us  [from_partner(): return lax.ppermute(value, axis, pairs)]
    scatter x1 -> x0, local copies, waits for them, and re-layouts: 9.35 us -> none  [routed_rows(): x_buf = jnp.zeros((peers * capacity, width), jnp.bfloat16).at[position].s...]
    another operation x4 -> x1, other arithmetic: 11.2 us -> 2.1 us
    reshape x2 -> x0, local copies, waits for them, and re-layouts: 8.79 us -> none  [the longest x1 7.32 us: routed_rows(): x_buf = jnp.zeros((peers * capacity, width), jnp.bfloat16).at[position].s...]
    dot_general x2 -> x5, matrix products: 21.8 us -> 28.7 us  [the longest x1 11.2 us: body(): jnp.dot(rows_in, lax.all_gather(weight, 'dp', axis=1, tiled=True)[0], pre...]
    scatter x1 -> x0, other arithmetic: 6.11 us -> none  [routed_rows(): g_buf = jnp.zeros((peers * capacity, grad_width), jnp.bfloat16).at[positi...]
  transfers between devices with their start and end apart: 5 -> 5, of which waited for: 4 -> 4; matrix products, arithmetic and copies ran while one was open for 15% -> 5% of each run, Pallas kernels for 0% -> 0%
where the time goes in v1:
time: 297 us; the launch traced here: 294 us
  waiting for transfers between devices  209 us (70%)
  matrix products  28.7 us (10%)
  starting transfers between devices  21.1 us (7%)
  between operations  14.1 us (5%)
  other arithmetic  11.2 us (4%)
  local copies, waits for them, and re-layouts  9.39 us (3%)
    reduce_scatter x1, waiting for transfers between devices, body(): lax.psum_scatter(lax.dot_general(rows_in, delta, contract, preferred_elem...  83 us
    all_to_all x1, waiting for transfers between devices, body(): lax.all_to_all(x_buf, 'expert', split_axis=0, concat_axis=0, tiled=True)  81 us
    all_to_all x1, waiting for transfers between devices, body(): lax.all_to_all(g_buf, 'expert', split_axis=0, concat_axis=0, tiled=True)  31.3 us
    ppermute x1, waiting for transfers between devices, from_partner(): return lax.ppermute(value, axis, pairs)  13.2 us
    all_to_all x1, starting transfers between devices, body(): lax.all_to_all(x_buf, 'expert', split_axis=0, concat_axis=0, tiled=True)  12.2 us
    dot_general x1, matrix products, body(): jnp.dot(rows_in, lax.all_gather(weight, 'dp', axis=1, tiled=True)[0], pre...  11.2 us
    dot_general x1, matrix products, body(): lax.dot_general(rows_in, delta, contract, preferred_element_type=jnp.floa...  10.6 us
    all_to_all x1, starting transfers between devices, body(): lax.all_to_all(g_buf, 'expert', split_axis=0, concat_axis=0, tiled=True)  8.61 us
  transfers between devices with their start and end apart: 5, of which 4 were waited for; matrix products, arithmetic and copies ran while one was open for 5% of the time, Pallas kernels for 0%

profile of v1, /device:TPU:28, one launch (start us, length us, event | category | flops | bytes accessed | tf_op | source)
XLA Modules:
  0.0 293.7 jit_solution(2817981643466192034)
XLA Ops:
  6.5 0.0 copy-start
  6.5 0.8 select_reduce_fusion.2
  7.4 0.1 fusion.17
  7.4 0.1 fusion.12
  7.6 0.7 select_reduce_fusion.1
  8.3 0.3 select_reduce_fusion
  8.6 2.9 multiply_convert_fusion
  11.5 8.6 %all-to-all-start.1 = ((bf16[32,36,768]{2,1,0:T(8,128)(2,1)}), bf16[32,36,768]{2,1,0:T(8,128)(2,1)S(1)}, u32[]{:S(2)}, u32[]{:S(2)}) async-start(bf16[32,36,768]{2,1,0:T(8,128)(2,1)} %multiply_convert_fusion), calls=%async_computation.1 | async-start | bytes 3932160 | tf_op jit(solution)/shard_map/all_to_all | solution.py:53
  20.1 0.0 all-gather.2.cloned.1.call-start
  20.2 0.7 all-gather.2.cloned.1.call-update
  20.9 0.0 copy-done
  20.9 3.8 %convolution_convert_fusion.1 = bf16[32,36,2048]{2,1,0:T(8,128)(2,1)} fusion(bf16[128,2048]{1,0:T(8,128)(2,1)S(1)} %copy-done, s32[32,128]{1,0:T(8,128)S(1)} %fusion.12), kind=kOutput, calls=%fused_computation.3 | convolution fusion | flops 606486528 | bytes 5259264 | tf_op jit(solution)/shard_map/brt,td->brd/dot_general | solution.py:31
  24.6 31.3 %all-to-all-done.1 = bf16[32,36,768]{2,1,0:T(8,128)(2,1)S(1)} async-done(((bf16[32,36,768]{2,1,0:T(8,128)(2,1)}), bf16[32,36,768]{2,1,0:T(8,128)(2,1)S(1)}, u32[]{:S(2)}, u32[]{:S(2)}) %all-to-all-start.1) | async-done | bytes 1769504 | tf_op jit(solution)/shard_map/all_to_all | solution.py:53
  56.0 12.2 %all-to-all-start = ((bf16[32,36,2048]{2,1,0:T(8,128)(2,1)}), bf16[32,36,2048]{2,1,0:T(8,128)(2,1)}, u32[]{:S(2)}, u32[]{:S(2)}) async-start(bf16[32,36,2048]{2,1,0:T(8,128)(2,1)} %convolution_convert_fusion.1), calls=%async_computation | async-start | bytes 10485760 | tf_op jit(solution)/shard_map/all_to_all | solution.py:52
  68.2 0.2 reduce-scatter.2.cloned.1.call-start
  68.4 1.9 reshape.19
  70.3 81.0 %all-to-all-done = bf16[32,36,2048]{2,1,0:T(8,128)(2,1)} async-done(((bf16[32,36,2048]{2,1,0:T(8,128)(2,1)}), bf16[32,36,2048]{2,1,0:T(8,128)(2,1)}, u32[]{:S(2)}, u32[]{:S(2)}) %all-to-all-start) | async-done | bytes 4718624 | tf_op jit(solution)/shard_map/all_to_all | solution.py:52
  151.4 7.2 %reshape.18 = bf16[1152,2048]{1,0:T(8,128)(2,1)} reshape(bf16[32,36,2048]{2,1,0:T(8,128)(2,1)} %all-to-all-done) | data formatting | bytes 9437184 | tf_op jit(solution)/shard_map/reshape | solution.py:55
  158.6 11.2 %fusion = f32[1152,1536]{1,0:T(8,128)S(1)} fusion(bf16[1152,2048]{1,0:T(8,128)(2,1)} %reshape.18, bf16[1,2048,1536]{2,1,0:T(8,128)(2,1)} %all-gather.2.cloned.1.call-done), kind=kOutput, calls=%fused_computation.1 | convolution fusion | flops 7247757312 | bytes 18087936 | tf_op jit(solution)/shard_map/dot_general | solution.py:57
  169.8 0.0 copy-done.1
  169.8 0.0 copy-start.2
  169.8 2.1 fusion.3
  171.9 0.2 copy-done.2
  172.2 10.6 %convolution_convert_fusion = bf16[2048,1536]{1,0:T(8,128)(2,1)} fusion(bf16[1152,2048]{1,0:T(8,128)(2,1)S(1)} %copy-done.2, bf16[1152,768]{1,0:T(8,128)(2,1)S(1)} %get-tuple-element.6, bf16[1152,768]{1,0:T(8,128)(2,1)S(1)} %get-tuple-element.5), kind=kOutput, calls=%fused_computation | convolution fusion | flops 7257980928 | bytes 14548992 | tf_op jit(solution)/shard_map/dot_general | solution.py:73
  182.8 0.0 reduce-scatter.2.cloned.1.call-update
  182.8 0.0 copy-start.6
  182.8 83.0 %reduce-scatter.2.cloned.1.call-done = bf16[256,1536]{1,0:T(8,128)(2,1)} async-done(((bf16[2048,1536]{1,0:T(8,128)(2,1)}), bf16[256,1536]{1,0:T(8,128)(2,1)}) %reduce-scatter.2.cloned.1.call-update) | async-done | bytes 786448 | tf_op jit(solution)/shard_map/reduce_scatter | solution.py:72
  265.8 3.1 %fusion.20 = bf16[256,1536]{1,0:T(8,128)(2,1)} fusion(bf16[1,256,1536]{2,1,0:T(8,128)(2,1)S(1)} %copy-done.3, bf16[256,1536]{1,0:T(8,128)(2,1)} %reduce-scatter.2.cloned.1.call-done, bf16[1,256,1536]{2,1,0:T(8,128)(2,1)S(1)} %copy-done.4), kind=kLoop, calls=%fused_computation.38 | loop fusion | flops 5111808 | bytes 3145728 | tf_op jit(solution)/shard_map/convert_element_type | solution.py:83
  268.9 0.0 collective-permute-start
  268.9 0.7 fusion.18
  270.2 13.2 %collective-permute-done = bf16[256,1536]{1,0:T(8,128)(2,1)} collective-permute-done((bf16[256,1536]{1,0:T(8,128)(2,1)}, bf16[256,1536]{1,0:T(8,128)(2,1)}, u32[]{:S(2)}, u32[]{:S(2)}) %collective-permute-start) | collective-permute-done | bytes 786464 | tf_op jit(solution)/shard_map/ppermute | solution.py:14
  283.5 3.4 %select_bitcast_fusion = f32[1,256,1536]{2,1,0:T(8,128)} fusion(bf16[256,1536]{1,0:T(8,128)(2,1)} %collective-permute-done, pred[]{:T(512)S(6)} %ne.3, bf16[1,256,1536]{2,1,0:T(8,128)(2,1)S(1)} %copy-done.3, bf16[256,1536]{1,0:T(8,128)(2,1)S(1)} %copy-done.5, bf16[1,256,1536]{2,1,0:T(8,128)(2,1)S(1)} %copy-done.4), kind=kLoop, calls=%fused_computation.20 | loop fusion | flops 5505024 | bytes 4718593 | tf_op jit(solution)/shard_map/broadcast_in_dim | solution.py:84
  (9 shorter events, 0.0 us)
Async XLA Ops:
  6.5 14.3 %copy-start = (bf16[128,2048]{1,0:T(8,128)(2,1)S(1)}, bf16[128,2048]{1,0:T(8,128)(2,1)}, u32[]{:S(2)}) copy-start(bf16[128,2048]{1,0:T(8,128)(2,1)} %param.9) | copy-start | bytes 1572868
  11.5 44.5 %all-to-all-start.1 = ((bf16[32,36,768]{2,1,0:T(8,128)(2,1)}), bf16[32,36,768]{2,1,0:T(8,128)(2,1)S(1)}, u32[]{:S(2)}, u32[]{:S(2)}) async-start(bf16[32,36,768]{2,1,0:T(8,128)(2,1)} %multiply_convert_fusion), calls=%async_computation.1 | async-start | bytes 3932160 | tf_op jit(solution)/shard_map/all_to_all | solution.py:53
  20.1 138.5 %all-gather.2.cloned.1.call-start = ((), (), s32[]{:S(2)}) async-start(), calls=%async_computation.3 | async-start | bytes 7077888 | tf_op jit(solution)/shard_map/all_gather | solution.py:59
  56.0 95.4 %all-to-all-start = ((bf16[32,36,2048]{2,1,0:T(8,128)(2,1)}), bf16[32,36,2048]{2,1,0:T(8,128)(2,1)}, u32[]{:S(2)}, u32[]{:S(2)}) async-start(bf16[32,36,2048]{2,1,0:T(8,128)(2,1)} %convolution_convert_fusion.1), calls=%async_computation | async-start | bytes 10485760 | tf_op jit(solution)/shard_map/all_to_all | solution.py:52
  68.2 197.6 %reduce-scatter.2.cloned.1.call-start = ((), (), s32[]{:S(2)}) async-start(), calls=%async_computation.4 | async-start | bytes 7077888 | tf_op jit(solution)/shard_map/reduce_scatter | solution.py:72
  158.6 11.2 %copy-start.1 = (f32[1152,768]{1,0:T(8,128)S(1)}, f32[1152,768]{1,0:T(8,128)}, u32[]{:S(2)}) copy-start(f32[1152,768]{1,0:T(8,128)} %reshape.19) | copy-start | bytes 10616836
  169.8 2.3 copy-start.2
  182.8 83.0 %copy-start.3 = (bf16[1,256,1536]{2,1,0:T(8,128)(2,1)S(1)}, bf16[1,256,1536]{2,1,0:T(8,128)(2,1)}, u32[]{:S(2)}) copy-start(bf16[1,256,1536]{2,1,0:T(8,128)(2,1)} %param.17) | copy-start | bytes 2359300
  182.8 83.0 %copy-start.4 = (bf16[1,256,1536]{2,1,0:T(8,128)(2,1)S(1)}, bf16[1,256,1536]{2,1,0:T(8,128)(2,1)}, u32[]{:S(2)}) copy-start(bf16[1,256,1536]{2,1,0:T(8,128)(2,1)} %param.16) | copy-start | bytes 2359300
  182.8 86.1 %copy-start.6 = (s32[32]{0:T(128)S(1)}, s32[32]{0:T(128)}, u32[]{:S(2)}) copy-start(s32[32]{0:T(128)} %param.14) | copy-start | bytes 388
  265.8 17.7 %copy-start.5 = (bf16[256,1536]{1,0:T(8,128)(2,1)S(1)}, bf16[256,1536]{1,0:T(8,128)(2,1)}, u32[]{:S(2)}) copy-start(bf16[256,1536]{1,0:T(8,128)(2,1)} %reduce-scatter.2.cloned.1.call-done) | copy-start | bytes 2359300
  268.9 14.5 %collective-permute-start = (bf16[256,1536]{1,0:T(8,128)(2,1)}, bf16[256,1536]{1,0:T(8,128)(2,1)}, u32[]{:S(2)}, u32[]{:S(2)}) collective-permute-start(bf16[256,1536]{1,0:T(8,128)(2,1)} %fusion.20), channel_id=1, source_target_pairs={{0,16},{1,17},{2,18},{3,19},{4,20},{5,21},{6,22},{7,23},{8,24},{9,... | collective-permute-start | bytes 2359304 | tf_op jit(solution)/shard_map/ppermute | solution.py:14
Sparse Core Ops, SparseCore 0:
  22.8 93.4 all-gather.1
  182.9 82.8 reduce-scatter.1

commit v2 on v1

--- a/solution.py
+++ b/solution.py
@@ -14,12 +14,15 @@
     return lax.ppermute(value, axis, pairs)
 
 
-def routed_rows(tokens, grad_out, slots, gate_probs, peers, capacity):
-    count, width = tokens.shape
+def plane_gates(slots, gate_probs, peers):
     labels = jnp.arange(peers, dtype=jnp.int32)
     hit = slots[None, :, :] == labels[:, None, None]
-    chosen = jnp.any(hit, axis=2)
-    gates = jnp.sum(jnp.where(hit, gate_probs[None], 0.0), axis=2)
+    return jnp.sum(jnp.where(hit, gate_probs[None], 0.0), axis=2)
+
+
+def routed_rows(rows, gates, width, capacity):
+    peers, count = gates.shape
+    chosen = gates > 0.0
     before = jnp.arange(count)[:, None] < jnp.arange(count)[None, :]
     ranks = jnp.dot(
         chosen.astype(jnp.bfloat16), before.astype(jnp.bfloat16), preferred_element_type=jnp.float32
@@ -27,10 +30,11 @@
     ranks = jnp.where(chosen, ranks, -1)
     picks = ranks[:, None, :] == jnp.arange(capacity, dtype=jnp.int32)[None, :, None]
     row_gate = jnp.sum(jnp.where(picks, gates[:, None, :], 0.0), axis=2)
-    picks = picks.astype(jnp.bfloat16)
-    x_buf = jnp.einsum("brt,td->brd", picks, tokens, preferred_element_type=jnp.float32)
-    g_buf = jnp.einsum("brt,td->brd", picks, grad_out, preferred_element_type=jnp.float32)
-    return x_buf.astype(jnp.bfloat16), (g_buf * row_gate[:, :, None]).astype(jnp.bfloat16)
+    picks = picks.astype(jnp.bfloat16).reshape(peers * capacity, count)
+    buf = jnp.dot(picks, rows, preferred_element_type=jnp.float32)
+    is_grad = jnp.arange(rows.shape[1]) >= width
+    scale = jnp.where(is_grad[None, :], row_gate.reshape(-1)[:, None], 1.0)
+    return (buf * scale).astype(jnp.bfloat16).reshape(peers, capacity, -1)
 
 
 def body(
@@ -47,13 +51,26 @@
     labels = jnp.arange(expert_count, dtype=jnp.int32)
     moved = jnp.sum(jnp.where(labels == my_index, partner, 0)) != my_index
     slots = jnp.sum(jnp.where(expert_ids[:, :, None] == labels, owner, 0), axis=2)
-    x_buf, g_buf = routed_rows(tokens, grad_out, slots, gate_probs, peers, capacity)
-    x_recv, g_recv = (
-        lax.all_to_all(x_buf, "expert", split_axis=0, concat_axis=0, tiled=True),
-        lax.all_to_all(g_buf, "expert", split_axis=0, concat_axis=0, tiled=True),
+    half = peers // 2
+    upper = my_index >= half
+    gates = plane_gates(slots, gate_probs, peers)
+    low_gates, high_gates = gates[:half], gates[half:]
+    packed = jnp.concatenate([tokens, grad_out], axis=1)
+    other_rows = from_partner(packed, "expert", swap_bit)
+    other_gates = from_partner(jnp.where(upper, low_gates, high_gates), "expert", swap_bit)
+    other_rows, weight = lax.optimization_barrier((other_rows, weight))
+    buf = routed_rows(
+        jnp.concatenate([packed, other_rows], axis=0),
+        jnp.concatenate([jnp.where(upper, high_gates, low_gates), other_gates], axis=1),
+        width,
+        2 * capacity,
     )
-    rows_in = x_recv.reshape(-1, width)
-    rows_grad = g_recv.reshape(-1, g_recv.shape[2])
+    planes = [list(range(half)), list(range(half, peers))]
+    recv = lax.all_to_all(
+        buf, "expert", split_axis=0, concat_axis=0, tiled=True, axis_index_groups=planes
+    ).reshape(half * 2 * capacity, -1)
+    rows_in = recv[:, :width]
+    rows_grad = recv[:, width:]
     pre_act = jnp.dot(
         rows_in,
         lax.all_gather(weight, "dp", axis=1, tiled=True)[0],

time: 297 us -> 247 us (0.83)
  waiting for transfers between devices: 209 us -> 114 us
  blocking collectives: 0 us -> 76.6 us
  starting transfers between devices: 21.1 us -> 3.88 us
  local copies, waits for them, and re-layouts: 9.39 us -> 2.25 us
  matrix products: 28.7 us -> 24 us
    all_to_all x2 -> x0, waiting for transfers between devices: 112 us -> none  [the longest x1 81 us: body(): lax.all_to_all(x_buf, 'expert', split_axis=0, concat_axis=0, tiled=True)]
    all_to_all x0 -> x1, blocking collectives: none -> 76.6 us  [body(): lax.all_to_all(buf, 'expert', split_axis=0, concat_axis=0, tiled=True, ax...]
    all_to_all x2 -> x0, starting transfers between devices: 20.8 us -> none  [the longest x1 12.2 us: body(): lax.all_to_all(x_buf, 'expert', split_axis=0, concat_axis=0, tiled=True)]
    ppermute x1 -> x3, waiting for transfers between devices: 13.2 us -> 31.1 us  [from_partner(): return lax.ppermute(value, axis, pairs)]
    reshape x1 -> x0, local copies, waits for them, and re-layouts: 7.22 us -> none  [body(): rows_in = x_recv.reshape(-1, width)]
    dot_general x2 -> x1, matrix products: 6.69 us -> 2.13 us  [routed_rows(): buf = jnp.dot(picks, rows, preferred_element_type=jnp.float32)]
    ppermute x1 -> x3, starting transfers between devices: 0.01 us -> 3.83 us  [from_partner(): return lax.ppermute(value, axis, pairs)]
  transfers between devices with their start and end apart: 5 -> 5, of which waited for: 4 -> 4; matrix products, arithmetic and copies ran while one was open for 5% -> 2% of each run, Pallas kernels for 0% -> 0%
where the time goes in v2:
time: 247 us; the launch traced here: 244 us
  waiting for transfers between devices  114 us (46%)
  blocking collectives  76.6 us (31%)
  matrix products  24 us (10%)
  between operations  14.2 us (6%)
  other arithmetic  8.89 us (4%)
  starting transfers between devices  3.88 us (2%)
    reduce_scatter x1, waiting for transfers between devices, body(): lax.psum_scatter(lax.dot_general(rows_in, delta, contract, preferred_elem...  83.3 us
    all_to_all x1, blocking collectives, body(): lax.all_to_all(buf, 'expert', split_axis=0, concat_axis=0, tiled=True, ax...  76.6 us
    ppermute x3, waiting for transfers between devices, from_partner(): return lax.ppermute(value, axis, pairs)  31.1 us
    dot_general x1, matrix products, body(): jnp.dot(rows_in, lax.all_gather(weight, 'dp', axis=1, tiled=True)[0], pre...  11.2 us
    dot_general x1, matrix products, body(): lax.dot_general(rows_in, delta, contract, preferred_element_type=jnp.floa...  10.5 us
  transfers between devices with their start and end apart: 5, of which 4 were waited for; matrix products, arithmetic and copies ran while one was open for 2% of the time, Pallas kernels for 0%

profile of v2, /device:TPU:28, one launch (start us, length us, event | category | flops | bytes accessed | tf_op | source)
XLA Modules:
  0.0 244.2 jit_solution(7802138204672105772)
XLA Ops:
  6.5 0.0 all-gather.2.cloned.1.call-start
  6.5 1.1 constant_dynamic-update-slice_fusion.1
  7.7 0.9 constant_dynamic-update-slice_fusion
  8.6 2.0 collective-permute-start.1
  10.6 16.1 %collective-permute-done.1 = bf16[128,2816]{1,0:T(8,128)(2,1)S(1)} collective-permute-done((bf16[128,2816]{1,0:T(8,128)(2,1)S(1)}, bf16[128,2816]{1,0:T(8,128)(2,1)S(1)}, u32[]{:S(2)}, u32[]{:S(2)}) %collective-permute-start.1) | collective-permute-done | bytes 720928 | tf_op jit(solution)/shard_map/ppermute | solution.py:14
  26.7 0.0 all-gather.2.cloned.1.call-update
  26.8 0.0 reduce-scatter.2.cloned.1.call-start
  26.8 0.0 copy-done.6
  26.8 0.0 copy-done.4
  26.8 0.1 select_reduce_fusion.2
  26.9 0.0 copy-done.5
  27.0 1.8 collective-permute-start
  28.9 0.1 eq.67
  28.9 1.8 collective-permute-done
  30.8 0.2 fusion.19
  30.9 0.4 select_reduce_fusion
  31.3 0.1 broadcast_in_dim.85
  31.4 0.2 bitcast_compare_fusion
  31.6 2.1 fusion
  33.7 76.6 %all_to_all.5 = bf16[16,72,2816]{2,1,0:T(8,128)(2,1)} all-to-all(bf16[16,72,2816]{2,1,0:T(8,128)(2,1)S(1)} %bitcast.25), channel_id=1, replica_groups={{0,1,2,3,4,5,6,7,8,9,10,11,12,13,14,15},{16,17,18,19,20,21,22,23,24,25,..., dimensions={0} | all-to-all | bytes 12976128 | tf_op jit(solution)/shard_map/all_to_all | solution.py:69
  110.3 11.2 %fusion.1 = f32[1152,1536]{1,0:T(8,128)S(1)} fusion(bf16[1,2048,1536]{2,1,0:T(8,128)(2,1)} %all-gather.2.cloned.1.call-done, bf16[1152,2816]{1,0:T(8,128)(2,1)} %bitcast.22), kind=kOutput, calls=%fused_computation.3 | convolution fusion | flops 7247757312 | bytes 18087936 | tf_op jit(solution)/shard_map/dot_general | solution.py:74
  121.5 0.0 copy-done
  121.5 2.1 fusion.6
  123.7 10.5 %convolution_convert_fusion = bf16[2048,1536]{1,0:T(8,128)(2,1)} fusion(bf16[1152,2816]{1,0:T(8,128)(2,1)S(1)} %bitcast.24, bf16[1152,768]{1,0:T(8,128)(2,1)S(1)} %get-tuple-element.10, bf16[1152,768]{1,0:T(8,128)(2,1)S(1)} %get-tuple-element.9), kind=kOutput, calls=%fused_computation.2 | convolution fusion | flops 7257980928 | bytes 14548992 | tf_op jit(solution)/shard_map/dot_general | solution.py:90
  134.2 0.0 reduce-scatter.2.cloned.1.call-update
  134.2 0.0 copy-start.7
  134.2 83.3 %reduce-scatter.2.cloned.1.call-done = bf16[256,1536]{1,0:T(8,128)(2,1)} async-done(((bf16[2048,1536]{1,0:T(8,128)(2,1)}), bf16[256,1536]{1,0:T(8,128)(2,1)}) %reduce-scatter.2.cloned.1.call-update) | async-done | bytes 786448 | tf_op jit(solution)/shard_map/reduce_scatter | solution.py:89
  217.5 3.1 %fusion.26 = bf16[256,1536]{1,0:T(8,128)(2,1)} fusion(bf16[1,256,1536]{2,1,0:T(8,128)(2,1)S(1)} %copy-done.1, bf16[256,1536]{1,0:T(8,128)(2,1)} %reduce-scatter.2.cloned.1.call-done, bf16[1,256,1536]{2,1,0:T(8,128)(2,1)S(1)} %copy-done.2), kind=kLoop, calls=%fused_computation.50 | loop fusion | flops 5111808 | bytes 3145728 | tf_op jit(solution)/shard_map/convert_element_type | solution.py:100
  220.6 0.0 collective-permute-start.2
  220.7 0.6 fusion.22
  221.9 13.2 %collective-permute-done.2 = bf16[256,1536]{1,0:T(8,128)(2,1)S(1)} collective-permute-done((bf16[256,1536]{1,0:T(8,128)(2,1)}, bf16[256,1536]{1,0:T(8,128)(2,1)S(1)}, u32[]{:S(2)}, u32[]{:S(2)}) %collective-permute-start.2) | collective-permute-done | bytes 786464 | tf_op jit(solution)/shard_map/ppermute | solution.py:14
  235.1 2.3 select_bitcast_fusion
  (17 shorter events, 0.1 us)
Async XLA Ops:
  6.5 20.3 %copy-start.6 = (s32[32]{0:T(128)S(1)}, s32[32]{0:T(128)}, u32[]{:S(2)}) copy-start(s32[32]{0:T(128)} %param.13) | copy-start | bytes 388
  6.5 20.3 %copy-start.4 = (s32[128,8]{0,1:T(8,128)S(1)}, s32[128,8]{0,1:T(8,128)}, u32[]{:S(2)}) copy-start(s32[128,8]{0,1:T(8,128)} %param.11) | copy-start | bytes 12292
  6.5 20.4 %copy-start.5 = (f32[128,8]{0,1:T(8,128)S(1)}, f32[128,8]{0,1:T(8,128)}, u32[]{:S(2)}) copy-start(f32[128,8]{0,1:T(8,128)} %param.12) | copy-start | bytes 12292
  6.5 103.8 %all-gather.2.cloned.1.call-start = ((), (), s32[]{:S(2)}) async-start(), calls=%async_computation.2 | async-start | bytes 7077888 | tf_op jit(solution)/shard_map/all_gather | solution.py:76
  8.6 18.1 %collective-permute-start.1 = (bf16[128,2816]{1,0:T(8,128)(2,1)S(1)}, bf16[128,2816]{1,0:T(8,128)(2,1)S(1)}, u32[]{:S(2)}, u32[]{:S(2)}) collective-permute-start(bf16[128,2816]{1,0:T(8,128)(2,1)S(1)} %constant_dynamic-update-slice_fusion), channel_id=1, source_target_pairs={{0,16},{1,17},{2,18},{3,19},{4,20},{5,21},{6,22},{7,23},{8,24},{9,... | collective-permute-start | bytes 2162696 | tf_op jit(solution)/shard_map/ppermute | solution.py:14
  26.8 190.7 %reduce-scatter.2.cloned.1.call-start = ((), (), s32[]{:S(2)}) async-start(), calls=%async_computation.3 | async-start | bytes 7077888 | tf_op jit(solution)/shard_map/reduce_scatter | solution.py:89
  27.0 3.7 %collective-permute-start = (f32[16,128]{1,0:T(8,128)S(1)}, f32[16,128]{1,0:T(8,128)S(1)}, u32[]{:S(2)}, u32[]{:S(2)}) collective-permute-start(f32[16,128]{1,0:T(8,128)S(1)} %get-tuple-element.12), channel_id=1, source_target_pairs={{0,16},{1,17},{2,18},{3,19},{4,20},{5,21},{6,22},{7,23},{8,24},{9,... | collective-permute-start | bytes 24584 | tf_op jit(solution)/shard_map/ppermute | solution.py:14
  110.3 11.2 %copy-start = (bf16[16,72,2816]{2,1,0:T(8,128)(2,1)S(1)}, bf16[16,72,2816]{2,1,0:T(8,128)(2,1)}, u32[]{:S(2)}) copy-start(bf16[16,72,2816]{2,1,0:T(8,128)(2,1)} %all_to_all.5) | copy-start | bytes 19464196
  134.2 83.3 %copy-start.1 = (bf16[1,256,1536]{2,1,0:T(8,128)(2,1)S(1)}, bf16[1,256,1536]{2,1,0:T(8,128)(2,1)}, u32[]{:S(2)}) copy-start(bf16[1,256,1536]{2,1,0:T(8,128)(2,1)} %param.17) | copy-start | bytes 2359300
  134.2 83.3 %copy-start.2 = (bf16[1,256,1536]{2,1,0:T(8,128)(2,1)S(1)}, bf16[1,256,1536]{2,1,0:T(8,128)(2,1)}, u32[]{:S(2)}) copy-start(bf16[1,256,1536]{2,1,0:T(8,128)(2,1)} %param.16) | copy-start | bytes 2359300
  134.2 86.4 %copy-start.7 = (s32[32]{0:T(128)S(1)}, s32[32]{0:T(128)}, u32[]{:S(2)}) copy-start(s32[32]{0:T(128)} %param.14) | copy-start | bytes 388
  217.5 17.6 %copy-start.3 = (bf16[256,1536]{1,0:T(8,128)(2,1)S(1)}, bf16[256,1536]{1,0:T(8,128)(2,1)}, u32[]{:S(2)}) copy-start(bf16[256,1536]{1,0:T(8,128)(2,1)} %reduce-scatter.2.cloned.1.call-done) | copy-start | bytes 2359300
  220.6 14.4 %collective-permute-start.2 = (bf16[256,1536]{1,0:T(8,128)(2,1)}, bf16[256,1536]{1,0:T(8,128)(2,1)S(1)}, u32[]{:S(2)}, u32[]{:S(2)}) collective-permute-start(bf16[256,1536]{1,0:T(8,128)(2,1)} %fusion.26), channel_id=1, source_target_pairs={{0,16},{1,17},{2,18},{3,19},{4,20},{5,21},{6,22},{7,23},{8,24},{9,... | collective-permute-start | bytes 2359304 | tf_op jit(solution)/shard_map/ppermute | solution.py:14
Sparse Core Ops, SparseCore 0:
  26.9 66.6 all-gather.1
  134.3 83.1 reduce-scatter.1

commit v3 on v2

--- a/solution.py
+++ b/solution.py
@@ -82,23 +82,36 @@
     sigma = jax.nn.sigmoid(gate_part)
     silu_value = gate_part * sigma
     slope = sigma * (1.0 + gate_part * (1.0 - sigma))
-    delta = jnp.concatenate([back * up_part * slope, back * silu_value], axis=1).astype(
-        jnp.bfloat16
+    contract = (((0,), (0,)), ((), ()))
+    first_old = first_moment[0].astype(jnp.float32)
+    second_old = second_moment[0].astype(jnp.float32)
+    deltas = lax.optimization_barrier(
+        ((back * up_part * slope).astype(jnp.bfloat16), (back * silu_value).astype(jnp.bfloat16))
     )
-    contract = (((0,), (0,)), ((), ()))
-    grads = lax.psum_scatter(
+    partials = [
         lax.dot_general(rows_in, delta, contract, preferred_element_type=jnp.float32).astype(
             jnp.bfloat16
-        ),
-        "dp",
-        scatter_dimension=0,
-        tiled=True,
-    ).astype(jnp.float32)
-    first_new = BETA_ONE * first_moment[0].astype(jnp.float32) + (1.0 - BETA_ONE) * grads
-    second_new = BETA_TWO * second_moment[0].astype(jnp.float32) + (1.0 - BETA_TWO) * grads * grads
-    step = first_new / (jnp.sqrt(second_new) + EPSILON)
-    arrived = from_partner(step.astype(jnp.bfloat16), "expert", swap_bit)
-    return jnp.where(moved, arrived.astype(jnp.float32), step)[None]
+        )
+        for delta in deltas
+    ]
+    outputs = []
+    arrived = None
+    for part in range(2):
+        columns = slice(part * width_hidden, (part + 1) * width_hidden)
+        grads = lax.psum_scatter(partials[part], "dp", scatter_dimension=0, tiled=True)
+        if part == 1:
+            grads, arrived = lax.optimization_barrier((grads, arrived))
+            outputs.append(jnp.where(moved, arrived.astype(jnp.float32), step))
+        grads = grads.astype(jnp.float32)
+        first_new = BETA_ONE * first_old[:, columns] + (1.0 - BETA_ONE) * grads
+        second_new = BETA_TWO * second_old[:, columns] + (1.0 - BETA_TWO) * grads * grads
+        step = first_new / (jnp.sqrt(second_new) + EPSILON)
+        sent = step.astype(jnp.bfloat16)
+        if part == 0:
+            sent, partials[1] = lax.optimization_barrier((sent, partials[1]))
+        arrived = from_partner(sent, "expert", swap_bit)
+    outputs.append(jnp.where(moved, arrived.astype(jnp.float32), step))
+    return jnp.concatenate(outputs, axis=1)[None]
 
 
 def solution(mesh):

time: 247 us -> 258 us (1.045)
  other arithmetic: 8.89 us -> 14.7 us
  matrix products: 24 us -> 28.3 us
  waiting for transfers between devices: 114 us -> 117 us
    convert_element_type x1 -> x4, other arithmetic: 3.13 us -> 9.5 us  [the longest x2 4.72 us: body(): sent = step.astype(jnp.bfloat16)]
    dot_general x1 -> x2, matrix products: 10.5 us -> 14.9 us  [body(): lax.dot_general(rows_in, delta, contract, preferred_element_type=jnp.floa...]
    reduce_scatter x1 -> x2, waiting for transfers between devices: 83.3 us -> 85.3 us  [body(): lax.psum_scatter(partials[part], 'dp', scatter_dimension=0, tiled=True)]
    ppermute x3 -> x4, waiting for transfers between devices: 31.1 us -> 31.2 us  [from_partner(): return lax.ppermute(value, axis, pairs)]
  transfers between devices with their start and end apart: 5 -> 7, of which waited for: 4 -> 6; matrix products, arithmetic and copies ran while one was open for 2% -> 7% of each run, Pallas kernels for 0% -> 0%
where the time goes in v3:
time: 258 us; the launch traced here: 256 us
  waiting for transfers between devices  117 us (45%)
  blocking collectives  76.6 us (30%)
  matrix products  28.3 us (11%)
  other arithmetic  14.7 us (6%)
  between operations  13.9 us (5%)
  starting transfers between devices  4.19 us (2%)
    reduce_scatter x2, waiting for transfers between devices, body(): lax.psum_scatter(partials[part], 'dp', scatter_dimension=0, tiled=True)  85.3 us
    all_to_all x1, blocking collectives, body(): lax.all_to_all(buf, 'expert', split_axis=0, concat_axis=0, tiled=True, ax...  76.6 us
    ppermute x4, waiting for transfers between devices, from_partner(): return lax.ppermute(value, axis, pairs)  31.2 us
    dot_general x2, matrix products, body(): lax.dot_general(rows_in, delta, contract, preferred_element_type=jnp.floa...  14.9 us
    dot_general x1, matrix products, body(): jnp.dot(rows_in, lax.all_gather(weight, 'dp', axis=1, tiled=True)[0], pre...  11.2 us
  transfers between devices with their start and end apart: 7, of which 6 were waited for; matrix products, arithmetic and copies ran while one was open for 7% of the time, Pallas kernels for 0%

profile of v3, /device:TPU:28, one launch (start us, length us, event | category | flops | bytes accessed | tf_op | source)
XLA Modules:
  0.0 256.5 jit_solution(15256765256620013227)
XLA Ops:
  6.5 1.1 constant_dynamic-update-slice_fusion.1
  7.6 0.9 constant_dynamic-update-slice_fusion
  8.6 2.0 collective-permute-start.1
  10.6 16.1 %collective-permute-done.1 = bf16[128,2816]{1,0:T(8,128)(2,1)S(1)} collective-permute-done((bf16[128,2816]{1,0:T(8,128)(2,1)S(1)}, bf16[128,2816]{1,0:T(8,128)(2,1)S(1)}, u32[]{:S(2)}, u32[]{:S(2)}) %collective-permute-start.1) | collective-permute-done | bytes 720928 | tf_op jit(solution)/shard_map/ppermute | solution.py:14
  26.8 0.8 select_reduce_fusion.2
  27.6 0.7 select_reduce_fusion.1
  28.3 1.8 collective-permute-start
  30.2 0.1 eq.67
  30.3 1.8 collective-permute-done
  32.1 0.2 fusion.20
  32.2 0.4 select_reduce_fusion
  32.6 0.1 broadcast_in_dim.85
  32.7 0.2 bitcast_compare_fusion
  32.9 2.1 fusion
  35.1 76.6 %all_to_all.5 = bf16[16,72,2816]{2,1,0:T(8,128)(2,1)} all-to-all(bf16[16,72,2816]{2,1,0:T(8,128)(2,1)S(1)} %bitcast.22), channel_id=1, replica_groups={{0,1,2,3,4,5,6,7,8,9,10,11,12,13,14,15},{16,17,18,19,20,21,22,23,24,25,..., dimensions={0} | all-to-all | bytes 12976128 | tf_op jit(solution)/shard_map/all_to_all | solution.py:69
  111.6 11.2 %fusion.1 = f32[1152,1536]{1,0:T(8,128)S(1)} fusion(bf16[1,2048,1536]{2,1,0:T(8,128)(2,1)} %all-gather.2.cloned.1.call-done, bf16[1152,2816]{1,0:T(8,128)(2,1)} %bitcast.18), kind=kOutput, calls=%fused_computation.2 | convolution fusion | flops 7247757312 | bytes 18087936 | tf_op jit(solution)/shard_map/dot_general | solution.py:74
  122.8 3.0 %fusion.10 = (bf16[1152,768]{1,0:T(8,128)(2,1)}, bf16[1152,768]{1,0:T(8,128)(2,1)S(1)}) fusion(f32[1152,1536]{1,0:T(8,128)S(1)} %fusion.1, bf16[1152,2816]{1,0:T(8,128)(2,1)S(1)} %bitcast.20), kind=kLoop, calls=%fused_computation.13 | loop fusion | flops 12386304 | bytes 12386304 | tf_op jit(solution)/shard_map/convert_element_type | solution.py:89
  125.8 5.9 %fusion.11 = bf16[2048,768]{1,0:T(8,128)(2,1)} fusion(bf16[1152,768]{1,0:T(8,128)(2,1)S(1)} %get-tuple-element.15, bf16[1152,2816]{1,0:T(8,128)(2,1)S(1)} %bitcast.21), kind=kOutput, calls=%fused_computation.15 | convolution fusion | flops 3625451520 | bytes 9633792 | tf_op jit(solution)/shard_map/dot_general | solution.py:92
  131.7 0.2 reduce-scatter.5.cloned.1.call-start
  132.0 1.8 bitcast_convert_fusion
  133.7 9.0 %fusion.14 = bf16[2048,768]{1,0:T(8,128)(2,1)} fusion(bf16[1152,768]{1,0:T(8,128)(2,1)} %get-tuple-element.16, bf16[1152,2816]{1,0:T(8,128)(2,1)} %bitcast.19), kind=kOutput, calls=%fused_computation.16 | convolution fusion | flops 3625451520 | bytes 9633792 | tf_op jit(solution)/shard_map/dot_general | solution.py:92
  142.7 43.1 %reduce-scatter.3.cloned.1.call-done = bf16[256,768]{1,0:T(8,128)(2,1)} async-done(((bf16[2048,768]{1,0:T(8,128)(2,1)}), bf16[256,768]{1,0:T(8,128)(2,1)}) %reduce-scatter.3.cloned.1.call-update) | async-done | bytes 393232 | tf_op jit(solution)/shard_map/reduce_scatter | solution.py:101
  185.8 2.4 fusion.38
  188.2 0.1 collective-permute-start.2
  188.3 7.9 %collective-permute-done.2 = bf16[256,768]{1,0:T(8,128)(2,1)} collective-permute-done((bf16[256,768]{1,0:T(8,128)(2,1)S(1)}, bf16[256,768]{1,0:T(8,128)(2,1)}, u32[]{:S(2)}, u32[]{:S(2)}) %collective-permute-start.2) | collective-permute-done | bytes 393248 | tf_op jit(solution)/shard_map/ppermute | solution.py:14
  196.1 42.3 %reduce-scatter.5.cloned.1.call-done = bf16[256,768]{1,0:T(8,128)(2,1)} async-done(((bf16[2048,768]{1,0:T(8,128)(2,1)}), bf16[256,768]{1,0:T(8,128)(2,1)}) %reduce-scatter.5.cloned.1.call-update) | async-done | bytes 393232 | tf_op jit(solution)/shard_map/reduce_scatter | solution.py:101
  238.4 2.4 fusion.36
  240.8 0.7 fusion.33
  242.1 1.1 convert_select_fusion.1
  243.2 5.4 %collective-permute-done.3 = bf16[256,768]{1,0:T(8,128)(2,1)S(1)} collective-permute-done((bf16[256,768]{1,0:T(8,128)(2,1)S(1)}, bf16[256,768]{1,0:T(8,128)(2,1)S(1)}, u32[]{:S(2)}, u32[]{:S(2)}) %collective-permute-start.3) | collective-permute-done | bytes 393248 | tf_op jit(solution)/shard_map/ppermute | solution.py:14
  248.6 0.1 convert_select_fusion
  248.6 1.3 maximum_bitcast_fusion
  (15 shorter events, 0.1 us)
Async XLA Ops:
  6.5 105.1 %all-gather.2.cloned.1.call-start = ((), (), s32[]{:S(2)}) async-start(), calls=%async_computation.3 | async-start | bytes 7077888 | tf_op jit(solution)/shard_map/all_gather | solution.py:76
  8.6 18.1 %collective-permute-start.1 = (bf16[128,2816]{1,0:T(8,128)(2,1)S(1)}, bf16[128,2816]{1,0:T(8,128)(2,1)S(1)}, u32[]{:S(2)}, u32[]{:S(2)}) collective-permute-start(bf16[128,2816]{1,0:T(8,128)(2,1)S(1)} %constant_dynamic-update-slice_fusion), channel_id=1, source_target_pairs={{0,16},{1,17},{2,18},{3,19},{4,20},{5,21},{6,22},{7,23},{8,24},{9,... | collective-permute-start | bytes 2162696 | tf_op jit(solution)/shard_map/ppermute | solution.py:14
  26.7 159.1 %reduce-scatter.3.cloned.1.call-start = ((), (), s32[]{:S(2)}) async-start(), calls=%async_computation.4 | async-start | bytes 3538944 | tf_op jit(solution)/shard_map/reduce_scatter | solution.py:101
  28.3 3.7 %collective-permute-start = (f32[16,128]{1,0:T(8,128)S(1)}, f32[16,128]{1,0:T(8,128)S(1)}, u32[]{:S(2)}, u32[]{:S(2)}) collective-permute-start(f32[16,128]{1,0:T(8,128)S(1)} %get-tuple-element.28), channel_id=1, source_target_pairs={{0,16},{1,17},{2,18},{3,19},{4,20},{5,21},{6,22},{7,23},{8,24},{9,... | collective-permute-start | bytes 24584 | tf_op jit(solution)/shard_map/ppermute | solution.py:14
  111.6 11.2 %copy-start = (bf16[16,72,2816]{2,1,0:T(8,128)(2,1)S(1)}, bf16[16,72,2816]{2,1,0:T(8,128)(2,1)}, u32[]{:S(2)}) copy-start(bf16[16,72,2816]{2,1,0:T(8,128)(2,1)} %all_to_all.5) | copy-start | bytes 19464196
  131.7 106.7 %reduce-scatter.5.cloned.1.call-start = ((), (), s32[]{:S(2)}) async-start(), calls=%async_computation.5 | async-start | bytes 3538944 | tf_op jit(solution)/shard_map/reduce_scatter | solution.py:101
  188.1 52.6 %copy-start.1 = (s32[32]{0:T(128)S(1)}, s32[32]{0:T(128)}, u32[]{:S(2)}) copy-start(s32[32]{0:T(128)} %param.14) | copy-start | bytes 388
  188.2 8.0 %collective-permute-start.2 = (bf16[256,768]{1,0:T(8,128)(2,1)S(1)}, bf16[256,768]{1,0:T(8,128)(2,1)}, u32[]{:S(2)}, u32[]{:S(2)}) collective-permute-start(bf16[256,768]{1,0:T(8,128)(2,1)S(1)} %get-tuple-element.18), channel_id=1, source_target_pairs={{0,16},{1,17},{2,18},{3,19},{4,20},{5,21},{6,22},{7,23},{8,24},{9,... | collective-permute-start | bytes 1179656 | tf_op jit(solution)/shard_map/ppermute | solution.py:14
  240.8 7.8 %collective-permute-start.3 = (bf16[256,768]{1,0:T(8,128)(2,1)S(1)}, bf16[256,768]{1,0:T(8,128)(2,1)S(1)}, u32[]{:S(2)}, u32[]{:S(2)}) collective-permute-start(bf16[256,768]{1,0:T(8,128)(2,1)S(1)} %get-tuple-element.21), channel_id=1, source_target_pairs={{0,16},{1,17},{2,18},{3,19},{4,20},{5,21},{6,22},{7,23},{8,24},{9,... | collective-permute-start | bytes 1179656 | tf_op jit(solution)/shard_map/ppermute | solution.py:14
Sparse Core Ops, SparseCore 0:
  26.8 66.4 all-gather.1
  131.9 53.8 reduce-scatter.2
  188.3 50.0 reduce-scatter.4

commit v4 on v2

--- a/solution.py
+++ b/solution.py
@@ -35,6 +35,31 @@
     is_grad = jnp.arange(rows.shape[1]) >= width
     scale = jnp.where(is_grad[None, :], row_gate.reshape(-1)[:, None], 1.0)
     return (buf * scale).astype(jnp.bfloat16).reshape(peers, capacity, -1)
+
+
+def ring_sum(rows_in, delta, way):
+    devices = lax.axis_size("dp")
+    chips = devices // 2
+    height = rows_in.shape[1] // devices
+    index = lax.axis_index("dp")
+    chip, core = index // 2, index % 2
+    swap = [(source, source ^ 1) for source in range(devices)]
+    onward = [(source, (source + 2 * way) % devices) for source in range(devices)]
+
+    def product(owner):
+        rows = lax.dynamic_slice_in_dim(rows_in, owner * height, height, axis=1)
+        contract = (((0,), (0,)), ((), ()))
+        return lax.dot_general(rows, delta, contract, preferred_element_type=jnp.float32)
+
+    total = None
+    for hop in range(chips):
+        target = (chip - way * (hop + 1)) % chips
+        theirs = product(2 * target + 1 - core).astype(jnp.bfloat16)
+        term = product(2 * target + core) + lax.ppermute(theirs, "dp", swap).astype(jnp.float32)
+        if total is not None:
+            term += lax.ppermute(total, "dp", onward).astype(jnp.float32)
+        total = term.astype(jnp.bfloat16)
+    return term
 
 
 def body(
@@ -82,18 +107,12 @@
     sigma = jax.nn.sigmoid(gate_part)
     silu_value = gate_part * sigma
     slope = sigma * (1.0 + gate_part * (1.0 - sigma))
-    delta = jnp.concatenate([back * up_part * slope, back * silu_value], axis=1).astype(
-        jnp.bfloat16
+    deltas = lax.optimization_barrier(
+        ((back * up_part * slope).astype(jnp.bfloat16), (back * silu_value).astype(jnp.bfloat16))
     )
-    contract = (((0,), (0,)), ((), ()))
-    grads = lax.psum_scatter(
-        lax.dot_general(rows_in, delta, contract, preferred_element_type=jnp.float32).astype(
-            jnp.bfloat16
-        ),
-        "dp",
-        scatter_dimension=0,
-        tiled=True,
-    ).astype(jnp.float32)
+    grads = jnp.concatenate(
+        [ring_sum(rows_in, deltas[0], 1), ring_sum(rows_in, deltas[1], -1)], axis=1
+    )
     first_new = BETA_ONE * first_moment[0].astype(jnp.float32) + (1.0 - BETA_ONE) * grads
     second_new = BETA_TWO * second_moment[0].astype(jnp.float32) + (1.0 - BETA_TWO) * grads * grads
     step = first_new / (jnp.sqrt(second_new) + EPSILON)

time: 247 us -> 259 us (1.049); the launches traced: 244 us -> 259 us
  blocking collectives: 76.6 us -> 0 us
  waiting for transfers between devices: 114 us -> 178 us
  starting transfers between devices: 3.88 us -> 24.7 us
  local copies, waits for them, and re-layouts: 2.25 us -> 7.57 us
  matrix products: 24 us -> 26.6 us
    all_to_all x0 -> x1, waiting for transfers between devices: none -> 92.9 us  [body(): lax.all_to_all(buf, 'expert', split_axis=0, concat_axis=0, tiled=True, ax...]
    reduce_scatter x1 -> x0, waiting for transfers between devices: 83.3 us -> none  [body(): lax.psum_scatter(lax.dot_general(rows_in, delta, contract, preferred_elem...]
    all_to_all x1 -> x0, blocking collectives: 76.6 us -> none  [body(): lax.all_to_all(buf, 'expert', split_axis=0, concat_axis=0, tiled=True, ax...]
    ppermute x0 -> x14, waiting for transfers between devices: none -> 52.3 us  [the longest x6 52.2 us: ring_sum(): term += lax.ppermute(total, 'dp', onward).astype(jnp.float32)]
    ppermute x0 -> x14, starting transfers between devices: none -> 11.8 us  [the longest x6 9.71 us: ring_sum(): term += lax.ppermute(total, 'dp', onward).astype(jnp.float32)]
    all_to_all x0 -> x1, starting transfers between devices: none -> 7.11 us  [body(): lax.all_to_all(buf, 'expert', split_axis=0, concat_axis=0, tiled=True, ax...]
    slice x0 -> x1, local copies, waits for them, and re-layouts: none -> 5.31 us  [body(): rows_in = recv[:, :width]]
    convert_element_type x0 -> x5, other arithmetic: none -> 3.9 us  [the longest x1 3.41 us: body(): (back * silu_value).astype(jnp.bfloat16)]
  transfers between devices with their start and end apart: 5 -> 19, of which waited for: 4 -> 10; matrix products, arithmetic and copies ran while one was open for 2% -> 9% of each run, Pallas kernels for 0% -> 0%
where the time goes in v4:
time: 259 us
  waiting for transfers between devices  178 us (69%)
  matrix products  26.6 us (10%)
  starting transfers between devices  24.7 us (10%)
  between operations  14.4 us (6%)
  other arithmetic  7.81 us (3%)
  local copies, waits for them, and re-layouts  7.57 us (3%)
    all_to_all x1, waiting for transfers between devices, body(): lax.all_to_all(buf, 'expert', split_axis=0, concat_axis=0, tiled=True, ax...  92.9 us
    ppermute x6, waiting for transfers between devices, ring_sum(): term += lax.ppermute(total, 'dp', onward).astype(jnp.float32)  52.2 us
    ppermute x3, waiting for transfers between devices, from_partner(): return lax.ppermute(value, axis, pairs)  32.9 us
    dot_general x16, matrix products, product(): lax.dot_general(rows, delta, contract, preferred_element_type=jnp.float32)  11.6 us
    dot_general x1, matrix products, body(): jnp.dot(rows_in, lax.all_gather(weight, 'dp', axis=1, tiled=True)[0], pre...  11 us
    ppermute x6, starting transfers between devices, ring_sum(): term += lax.ppermute(total, 'dp', onward).astype(jnp.float32)  9.71 us
    all_to_all x1, starting transfers between devices, body(): lax.all_to_all(buf, 'expert', split_axis=0, concat_axis=0, tiled=True, ax...  7.11 us
    ppermute x3, starting transfers between devices, from_partner(): return lax.ppermute(value, axis, pairs)  5.81 us
  transfers between devices with their start and end apart: 19, of which 10 were waited for; matrix products, arithmetic and copies ran while one was open for 9% of the time, Pallas kernels for 0%

profile of v4, /device:TPU:28, one launch (start us, length us, event | category | flops | bytes accessed | tf_op | source)
XLA Modules:
  0.0 259.2 jit_solution(5683683621144111177)
XLA Ops:
  6.5 1.1 constant_dynamic-update-slice_fusion.1
  7.7 0.9 constant_dynamic-update-slice_fusion
  8.6 2.0 collective-permute-start.1
  10.6 16.1 %collective-permute-done.1 = bf16[128,2816]{1,0:T(8,128)(2,1)S(1)} collective-permute-done((bf16[128,2816]{1,0:T(8,128)(2,1)S(1)}, bf16[128,2816]{1,0:T(8,128)(2,1)S(1)}, u32[]{:S(2)}, u32[]{:S(2)}) %collective-permute-start.1) | collective-permute-done | bytes 720928 | tf_op jit(solution)/shard_map/ppermute | solution.py:14
  27.0 1.8 collective-permute-start
  28.9 1.8 collective-permute-done
  31.6 3.8 %fusion = bf16[1152,2816]{1,0:T(8,128)(2,1)} fusion(pred[1152,256]{1,0:T(32,128)(4,1)S(1)} %bitcast_compare_fusion, f32[1152]{0:T(1024)S(1)} %broadcast_in_dim.85, pred[2816]{0:T(1024)(128)(4,1)S(1)} %iota_compare_fusion.5, bf16[128,2816]{1,0:T(8,128)(2,1)S(1)} %collective-permute-done.1, bf16[128,2816]{1,0:T(8,128)(2,1)S(1)} %constant_dynamic-update-slice_fusion), kind=kOutput, calls=%fused_computation.1 | convolution fusion | flops 1673560064 | bytes 8232192 | tf_op jit(solution)/shard_map/dot_general | solution.py:34
  35.4 7.1 %all-to-all-start = ((bf16[16,72,2816]{2,1,0:T(8,128)(2,1)}), bf16[16,72,2816]{2,1,0:T(8,128)(2,1)}, u32[]{:S(2)}, u32[]{:S(2)}) async-start(bf16[16,72,2816]{2,1,0:T(8,128)(2,1)} %bitcast.34), calls=%async_computation | async-start | bytes 12976128 | tf_op jit(solution)/shard_map/all_to_all | solution.py:94
  42.5 92.9 %all-to-all-done = bf16[16,72,2816]{2,1,0:T(8,128)(2,1)} async-done(((bf16[16,72,2816]{2,1,0:T(8,128)(2,1)}), bf16[16,72,2816]{2,1,0:T(8,128)(2,1)}, u32[]{:S(2)}, u32[]{:S(2)}) %all-to-all-start) | async-done | bytes 6488096 | tf_op jit(solution)/shard_map/all_to_all | solution.py:94
  135.5 5.3 %slice.26 = bf16[1152,2048]{1,0:T(8,128)(2,1)} slice(bf16[1152,2816]{1,0:T(8,128)(2,1)} %bitcast.3), slice={[0:1152], [0:2048]} | slice | bytes 9437184 | tf_op jit(solution)/shard_map/slice | solution.py:97
  140.8 11.0 %fusion.1 = f32[1152,1536]{1,0:T(8,128)S(1)} fusion(bf16[1,2048,1536]{2,1,0:T(8,128)(2,1)} %all-gather.2.cloned.1.call-done, bf16[1152,2816]{1,0:T(8,128)(2,1)} %bitcast.3), kind=kOutput, calls=%fused_computation.2 | convolution fusion | flops 7247757312 | bytes 18087936 | tf_op jit(solution)/shard_map/dot_general | solution.py:99
  151.8 3.4 %fusion.5 = (bf16[1152,768]{1,0:T(8,128)(2,1)S(1)}, bf16[1152,768]{1,0:T(8,128)(2,1)S(1)}) fusion(f32[1152,1536]{1,0:T(8,128)S(1)} %fusion.1, bf16[1152,2816]{1,0:T(8,128)(2,1)} %bitcast.3), kind=kLoop, calls=%fused_computation.8 | loop fusion | flops 12386304 | bytes 12386304 | tf_op jit(solution)/shard_map/convert_element_type | solution.py:111
  156.8 0.7 convolution_convert_fusion.1
  157.5 0.8 collective-permute-start.11
  160.6 0.7 convolution_convert_fusion.3
  164.1 0.7 convolution_convert_fusion.5
  164.9 0.7 add_convert_fusion.2
  165.6 2.0 collective-permute-start.13
  168.3 1.4 collective-permute-start.6
  170.8 13.3 %collective-permute-done.13 = bf16[256,768]{1,0:T(8,128)(2,1)S(1)} collective-permute-done((bf16[256,768]{1,0:T(8,128)(2,1)S(1)}, bf16[256,768]{1,0:T(8,128)(2,1)S(1)}, u32[]{:S(2)}, u32[]{:S(2)}) %collective-permute-start.13) | collective-permute-done | bytes 393248 | tf_op jit(solution)/shard_map/ppermute | solution.py:60
  184.3 3.5 %collective-permute-start.14 = (bf16[256,768]{1,0:T(8,128)(2,1)S(1)}, bf16[256,768]{1,0:T(8,128)(2,1)S(1)}, u32[]{:S(2)}, u32[]{:S(2)}) collective-permute-start(bf16[256,768]{1,0:T(8,128)(2,1)S(1)} %add_convert_fusion.1), channel_id=1, source_target_pairs={{0,192},{32,224},{64,0},{96,32},{128,64},{160,96},{192,128},{224,1... | collective-permute-start | bytes 1179656 | tf_op jit(solution)/shard_map/ppermute | solution.py:60
  187.8 1.6 collective-permute-done.6
  189.5 1.1 collective-permute-start.7
  191.5 15.4 %collective-permute-done.14 = bf16[256,768]{1,0:T(8,128)(2,1)S(1)} collective-permute-done((bf16[256,768]{1,0:T(8,128)(2,1)S(1)}, bf16[256,768]{1,0:T(8,128)(2,1)S(1)}, u32[]{:S(2)}, u32[]{:S(2)}) %collective-permute-start.14) | collective-permute-done | bytes 393248 | tf_op jit(solution)/shard_map/ppermute | solution.py:60
  206.9 1.2 collective-permute-start.15
  208.1 2.0 collective-permute-done.7
  211.6 16.8 %collective-permute-done.15 = bf16[256,768]{1,0:T(8,128)(2,1)S(1)} collective-permute-done((bf16[256,768]{1,0:T(8,128)(2,1)S(1)}, bf16[256,768]{1,0:T(8,128)(2,1)S(1)}, u32[]{:S(2)}, u32[]{:S(2)}) %collective-permute-start.15) | collective-permute-done | bytes 393248 | tf_op jit(solution)/shard_map/ppermute | solution.py:60
  228.5 3.2 %collective-permute-done.8 = bf16[256,768]{1,0:T(8,128)(2,1)S(1)} collective-permute-done((bf16[256,768]{1,0:T(8,128)(2,1)S(1)}, bf16[256,768]{1,0:T(8,128)(2,1)S(1)}, u32[]{:S(2)}, u32[]{:S(2)}) %collective-permute-start.8) | collective-permute-done | bytes 393248 | tf_op jit(solution)/shard_map/ppermute | solution.py:60
  231.8 1.0 fusion.64
  232.8 2.0 collective-permute-start.16
  236.1 14.9 %collective-permute-done.16 = bf16[256,1536]{1,0:T(8,128)(2,1)S(1)} collective-permute-done((bf16[256,1536]{1,0:T(8,128)(2,1)S(1)}, bf16[256,1536]{1,0:T(8,128)(2,1)S(1)}, u32[]{:S(2)}, u32[]{:S(2)}) %collective-permute-start.16) | collective-permute-done | bytes 786464 | tf_op jit(solution)/shard_map/ppermute | solution.py:14
  251.0 1.3 select_bitcast_fusion
  (63 shorter events, 13.0 us)
Async XLA Ops:
  6.5 20.2 %copy-start.5 = (s32[32]{0:T(128)S(1)}, s32[32]{0:T(128)}, u32[]{:S(2)}) copy-start(s32[32]{0:T(128)} %param.13) | copy-start | bytes 388
  6.5 20.3 %copy-start.3 = (s32[128,8]{0,1:T(8,128)S(1)}, s32[128,8]{0,1:T(8,128)}, u32[]{:S(2)}) copy-start(s32[128,8]{0,1:T(8,128)} %param.11) | copy-start | bytes 12292
  6.5 20.4 %copy-start.4 = (f32[128,8]{0,1:T(8,128)S(1)}, f32[128,8]{0,1:T(8,128)}, u32[]{:S(2)}) copy-start(f32[128,8]{0,1:T(8,128)} %param.12) | copy-start | bytes 12292
  6.5 134.2 %all-gather.2.cloned.1.call-start = ((), (), s32[]{:S(2)}) async-start(), calls=%async_computation.1 | async-start | bytes 7077888 | tf_op jit(solution)/shard_map/all_gather | solution.py:101
  8.6 18.1 %collective-permute-start.1 = (bf16[128,2816]{1,0:T(8,128)(2,1)S(1)}, bf16[128,2816]{1,0:T(8,128)(2,1)S(1)}, u32[]{:S(2)}, u32[]{:S(2)}) collective-permute-start(bf16[128,2816]{1,0:T(8,128)(2,1)S(1)} %constant_dynamic-update-slice_fusion), channel_id=1, source_target_pairs={{0,16},{1,17},{2,18},{3,19},{4,20},{5,21},{6,22},{7,23},{8,24},{9,... | collective-permute-start | bytes 2162696 | tf_op jit(solution)/shard_map/ppermute | solution.py:14
  27.0 3.7 %collective-permute-start = (f32[16,128]{1,0:T(8,128)S(1)}, f32[16,128]{1,0:T(8,128)S(1)}, u32[]{:S(2)}, u32[]{:S(2)}) collective-permute-start(f32[16,128]{1,0:T(8,128)S(1)} %get-tuple-element.18), channel_id=1, source_target_pairs={{0,16},{1,17},{2,18},{3,19},{4,20},{5,21},{6,22},{7,23},{8,24},{9,... | collective-permute-start | bytes 24584 | tf_op jit(solution)/shard_map/ppermute | solution.py:14
  35.4 100.1 %all-to-all-start = ((bf16[16,72,2816]{2,1,0:T(8,128)(2,1)}), bf16[16,72,2816]{2,1,0:T(8,128)(2,1)}, u32[]{:S(2)}, u32[]{:S(2)}) async-start(bf16[16,72,2816]{2,1,0:T(8,128)(2,1)} %bitcast.34), calls=%async_computation | async-start | bytes 12976128 | tf_op jit(solution)/shard_map/all_to_all | solution.py:94
  151.8 3.4 %copy-start = (bf16[1152,2048]{1,0:T(8,128)(2,1)S(1)}, bf16[1152,2048]{1,0:T(8,128)(2,1)}, u32[]{:S(2)}) copy-start(bf16[1152,2048]{1,0:T(8,128)(2,1)} %slice.26) | copy-start | bytes 14155780
  156.0 8.9 %collective-permute-start.12 = (bf16[256,768]{1,0:T(8,128)(2,1)S(1)}, bf16[256,768]{1,0:T(8,128)(2,1)S(1)}, u32[]{:S(2)}, u32[]{:S(2)}) collective-permute-start(bf16[256,768]{1,0:T(8,128)(2,1)S(1)} %convolution_convert_fusion), channel_id=1, source_target_pairs={{0,32},{32,0},{64,96},{96,64},{128,160},{160,128},{192,224},{224,1... | collective-permute-start | bytes 1179656 | tf_op jit(solution)/shard_map/ppermute | solution.py:58
  157.5 12.9 %collective-permute-start.11 = (bf16[256,768]{1,0:T(8,128)(2,1)S(1)}, bf16[256,768]{1,0:T(8,128)(2,1)S(1)}, u32[]{:S(2)}, u32[]{:S(2)}) collective-permute-start(bf16[256,768]{1,0:T(8,128)(2,1)S(1)} %convolution_convert_fusion.1), channel_id=1, source_target_pairs={{0,32},{32,0},{64,96},{96,64},{128,160},{160,128},{192,224},{224,1... | collective-permute-start | bytes 1179656 | tf_op jit(solution)/shard_map/ppermute | solution.py:58
  159.8 31.6 %collective-permute-start.10 = (bf16[256,768]{1,0:T(8,128)(2,1)S(1)}, bf16[256,768]{1,0:T(8,128)(2,1)S(1)}, u32[]{:S(2)}, u32[]{:S(2)}) collective-permute-start(bf16[256,768]{1,0:T(8,128)(2,1)S(1)} %convolution_convert_fusion.2), channel_id=1, source_target_pairs={{0,32},{32,0},{64,96},{96,64},{128,160},{160,128},{192,224},{224,1... | collective-permute-start | bytes 1179656 | tf_op jit(solution)/shard_map/ppermute | solution.py:58
  162.0 5.6 %collective-permute-start.5 = (bf16[256,768]{1,0:T(8,128)(2,1)S(1)}, bf16[256,768]{1,0:T(8,128)(2,1)S(1)}, u32[]{:S(2)}, u32[]{:S(2)}) collective-permute-start(bf16[256,768]{1,0:T(8,128)(2,1)S(1)} %convolution_convert_fusion.4), channel_id=1, source_target_pairs={{0,32},{32,0},{64,96},{96,64},{128,160},{160,128},{192,224},{224,1... | collective-permute-start | bytes 1179656 | tf_op jit(solution)/shard_map/ppermute | solution.py:58
  164.8 19.5 %collective-permute-start.4 = (bf16[256,768]{1,0:T(8,128)(2,1)S(1)}, bf16[256,768]{1,0:T(8,128)(2,1)S(1)}, u32[]{:S(2)}, u32[]{:S(2)}) collective-permute-start(bf16[256,768]{1,0:T(8,128)(2,1)S(1)} %convolution_convert_fusion.5), channel_id=1, source_target_pairs={{0,32},{32,0},{64,96},{96,64},{128,160},{160,128},{192,224},{224,1... | collective-permute-start | bytes 1179656 | tf_op jit(solution)/shard_map/ppermute | solution.py:58
  165.6 18.4 %collective-permute-start.13 = (bf16[256,768]{1,0:T(8,128)(2,1)S(1)}, bf16[256,768]{1,0:T(8,128)(2,1)S(1)}, u32[]{:S(2)}, u32[]{:S(2)}) collective-permute-start(bf16[256,768]{1,0:T(8,128)(2,1)S(1)} %add_convert_fusion.2), channel_id=1, source_target_pairs={{0,192},{32,224},{64,0},{96,32},{128,64},{160,96},{192,128},{224,1... | collective-permute-start | bytes 1179656 | tf_op jit(solution)/shard_map/ppermute | solution.py:60
  168.3 21.0 %collective-permute-start.6 = (bf16[256,768]{1,0:T(8,128)(2,1)S(1)}, bf16[256,768]{1,0:T(8,128)(2,1)S(1)}, u32[]{:S(2)}, u32[]{:S(2)}) collective-permute-start(bf16[256,768]{1,0:T(8,128)(2,1)S(1)} %add_convert_fusion.5), channel_id=1, source_target_pairs={{0,64},{32,96},{64,128},{96,160},{128,192},{160,224},{192,0},{224,... | collective-permute-start | bytes 1179656 | tf_op jit(solution)/shard_map/ppermute | solution.py:60
  170.5 41.1 %collective-permute-start.9 = (bf16[256,768]{1,0:T(8,128)(2,1)S(1)}, bf16[256,768]{1,0:T(8,128)(2,1)S(1)}, u32[]{:S(2)}, u32[]{:S(2)}) collective-permute-start(bf16[256,768]{1,0:T(8,128)(2,1)S(1)} %convolution_convert_fusion.3), channel_id=1, source_target_pairs={{0,32},{32,0},{64,96},{96,64},{128,160},{160,128},{192,224},{224,1... | collective-permute-start | bytes 1179656 | tf_op jit(solution)/shard_map/ppermute | solution.py:58
  184.1 24.1 %collective-permute-start.3 = (bf16[256,768]{1,0:T(8,128)(2,1)S(1)}, bf16[256,768]{1,0:T(8,128)(2,1)S(1)}, u32[]{:S(2)}, u32[]{:S(2)}) collective-permute-start(bf16[256,768]{1,0:T(8,128)(2,1)S(1)} %convolution_convert_fusion.6), channel_id=1, source_target_pairs={{0,32},{32,0},{64,96},{96,64},{128,160},{160,128},{192,224},{224,1... | collective-permute-start | bytes 1179656 | tf_op jit(solution)/shard_map/ppermute | solution.py:58
  184.3 22.6 %collective-permute-start.14 = (bf16[256,768]{1,0:T(8,128)(2,1)S(1)}, bf16[256,768]{1,0:T(8,128)(2,1)S(1)}, u32[]{:S(2)}, u32[]{:S(2)}) collective-permute-start(bf16[256,768]{1,0:T(8,128)(2,1)S(1)} %add_convert_fusion.1), channel_id=1, source_target_pairs={{0,192},{32,224},{64,0},{96,32},{128,64},{160,96},{192,128},{224,1... | collective-permute-start | bytes 1179656 | tf_op jit(solution)/shard_map/ppermute | solution.py:60
  189.5 20.7 %collective-permute-start.7 = (bf16[256,768]{1,0:T(8,128)(2,1)S(1)}, bf16[256,768]{1,0:T(8,128)(2,1)S(1)}, u32[]{:S(2)}, u32[]{:S(2)}) collective-permute-start(bf16[256,768]{1,0:T(8,128)(2,1)S(1)} %add_convert_fusion.4), channel_id=1, source_target_pairs={{0,64},{32,96},{64,128},{96,160},{128,192},{160,224},{192,0},{224,... | collective-permute-start | bytes 1179656 | tf_op jit(solution)/shard_map/ppermute | solution.py:60
  191.4 37.1 %collective-permute-start.2 = (bf16[256,768]{1,0:T(8,128)(2,1)S(1)}, bf16[256,768]{1,0:T(8,128)(2,1)S(1)}, u32[]{:S(2)}, u32[]{:S(2)}) collective-permute-start(bf16[256,768]{1,0:T(8,128)(2,1)S(1)} %convolution_convert_fusion.7), channel_id=1, source_target_pairs={{0,32},{32,0},{64,96},{96,64},{128,160},{160,128},{192,224},{224,1... | collective-permute-start | bytes 1179656 | tf_op jit(solution)/shard_map/ppermute | solution.py:58
  206.9 21.4 %collective-permute-start.15 = (bf16[256,768]{1,0:T(8,128)(2,1)S(1)}, bf16[256,768]{1,0:T(8,128)(2,1)S(1)}, u32[]{:S(2)}, u32[]{:S(2)}) collective-permute-start(bf16[256,768]{1,0:T(8,128)(2,1)S(1)} %add_convert_fusion), channel_id=1, source_target_pairs={{0,192},{32,224},{64,0},{96,32},{128,64},{160,96},{192,128},{224,1... | collective-permute-start | bytes 1179656 | tf_op jit(solution)/shard_map/ppermute | solution.py:60
  210.3 21.4 %collective-permute-start.8 = (bf16[256,768]{1,0:T(8,128)(2,1)S(1)}, bf16[256,768]{1,0:T(8,128)(2,1)S(1)}, u32[]{:S(2)}, u32[]{:S(2)}) collective-permute-start(bf16[256,768]{1,0:T(8,128)(2,1)S(1)} %add_convert_fusion.3), channel_id=1, source_target_pairs={{0,64},{32,96},{64,128},{96,160},{128,192},{160,224},{192,0},{224,... | collective-permute-start | bytes 1179656 | tf_op jit(solution)/shard_map/ppermute | solution.py:60
  228.5 3.3 %copy-start.1 = (bf16[1,256,1536]{2,1,0:T(8,128)(2,1)S(1)}, bf16[1,256,1536]{2,1,0:T(8,128)(2,1)}, u32[]{:S(2)}) copy-start(bf16[1,256,1536]{2,1,0:T(8,128)(2,1)} %param.17) | copy-start | bytes 2359300
  228.5 3.3 %copy-start.2 = (bf16[1,256,1536]{2,1,0:T(8,128)(2,1)S(1)}, bf16[1,256,1536]{2,1,0:T(8,128)(2,1)}, u32[]{:S(2)}) copy-start(bf16[1,256,1536]{2,1,0:T(8,128)(2,1)} %param.16) | copy-start | bytes 2359300
  231.8 3.0 %copy-start.6 = (s32[32]{0:T(128)S(1)}, s32[32]{0:T(128)}, u32[]{:S(2)}) copy-start(s32[32]{0:T(128)} %param.14) | copy-start | bytes 388
  232.8 18.2 %collective-permute-start.16 = (bf16[256,1536]{1,0:T(8,128)(2,1)S(1)}, bf16[256,1536]{1,0:T(8,128)(2,1)S(1)}, u32[]{:S(2)}, u32[]{:S(2)}) collective-permute-start(bf16[256,1536]{1,0:T(8,128)(2,1)S(1)} %get-tuple-element.13), channel_id=1, source_target_pairs={{0,16},{1,17},{2,18},{3,19},{4,20},{5,21},{6,22},{7,23},{8,24},{9,... | collective-permute-start | bytes 2359304 | tf_op jit(solution)/shard_map/ppermute | solution.py:14
Sparse Core Ops, SparseCore 0:
  26.9 72.7 all-gather.1
